TPU v7x, 32 devices: a whole 2x2x4 slice. The times are simulated.
32 devices in a mesh: dp: 16 (over z, y, x), rep: 2 (over core).
Axes of the slice: x: 2, y: 2, z: 4, core: 2. Of those that a mesh axis runs over, the one named last changes fastest.
Arguments:
- table: float32 [131072, 400], P(('dp', 'rep')), may hold values from -6 to 6
- batch_index: int32 [32768], P(('dp', 'rep')), may hold values from 0 to 4095
- labels: int32 [32768], P(('dp', 'rep')), may hold values from 0 to 46
- w_branch: float32 [4, 100, 512], P(None, None, 'dp'), may hold values from -0.625 to 0.625
- w_merge: float32 [2048, 512], P('dp'), may hold values from -0.125 to 0.125
- w_class: float32 [512, 47], P('dp'), may hold values from -0.5 to 0.5
- small_params: float32 [20, 512], P(None, 'dp'), as said below
- first_branch: float32 [4, 100, 512], P(None, None, 'dp'), may hold values from -0.0014648438 to 0.0014648438
- first_merge: float32 [2048, 512], P('dp'), may hold values from -0.0014648438 to 0.0014648438
- first_class: float32 [512, 47], P('dp'), may hold values from -0.0014648438 to 0.0014648438
- first_small: float32 [20, 512], P(None, 'dp'), may hold values from -0.00390625 to 0.00390625
- second_branch: float32 [4, 100, 512], P(None, None, 'dp'), may hold values from 7.7659046e-10 to 3.1063618e-09
- second_merge: float32 [2048, 512], P('dp'), may hold values from 7.7659046e-10 to 3.1063618e-09
- second_class: float32 [512, 47], P('dp'), may hold values from 7.7659046e-10 to 3.1063618e-09
- second_small: float32 [20, 512], P(None, 'dp'), may hold values from 6.989314e-09 to 2.7957256e-08
Outputs:
- new_branch: float32 [4, 100, 512], P(None, None, 'dp')
- new_merge: float32 [2048, 512], P('dp')
- new_class: float32 [512, 47], P('dp')
- new_small: float32 [20, 512], P(None, 'dp')
- moment_branch: float32 [4, 100, 512], P(None, None, 'dp')
- moment_merge: float32 [2048, 512], P('dp')
- moment_class: float32 [512, 47], P('dp')
- moment_small: float32 [20, 512], P(None, 'dp')
- square_branch: float32 [4, 100, 512], P(None, None, 'dp')
- square_merge: float32 [2048, 512], P('dp')
- square_class: float32 [512, 47], P('dp')
- square_small: float32 [20, 512], P(None, 'dp')
- copy_branch: bfloat16 [4, 100, 512], P(None, None, 'dp')
- copy_merge: bfloat16 [2048, 512], P('dp')
- copy_class: bfloat16 [512, 47], P('dp')
- copy_small: bfloat16 [20, 512], P(None, 'dp')
- grad_norm: float32 [], replicated
- row_grads: float32 [32768, 400], P(('dp', 'rep'))
Inputs may be any that keep to these rules, and one draw needn't show every extreme that they name: `batch_index`: each entry indexes a row of the block of 4096 table rows that lies on the same device as the entry. `small_params`: gains lie in 0.3 to 2.0, slopes in 0.05 to 0.45.
All inputs are finite; a program needn't handle non-finite values.
Results may differ from a plain program's by a relative error of at most 0.011.
Values may be sent and summed in bfloat16 or wider, within the bound.
No kernel may reach another device: no remote copies, remote signals or barrier semaphores. Data moves between devices by JAX's collectives and lax.ppermute only.
A program may use at most 128 MiB of HBM per device.

v0:
```python
import jax
import jax.numpy as jnp
from jax import lax
from jax.sharding import PartitionSpec as P

HOPS = 4
STEP = 7
EPS_NORM = 1e-05


def leaky(value, slope):
    return slope * value + (1.0 - slope) * value * jax.nn.sigmoid(value)


def leaky_back(upstream, value, slope):
    sig = jax.nn.sigmoid(value)
    slope_term = jnp.sum(upstream * value * (1.0 - sig), axis=0)
    derivative = slope + (1.0 - slope) * (sig + value * sig * (1.0 - sig))
    return (upstream * derivative, slope_term)


def cross_dot(left, right):
    return lax.dot_general(
        left, right, (((0,), (0,)), ((), ())), preferred_element_type=jnp.float32
    )


def back_dot(left, right):
    return lax.dot_general(
        left, right, (((1,), (1,)), ((), ())), preferred_element_type=jnp.float32
    )


def adamw(weight, grad, moment, square, scale, rate):
    clipped = grad * scale
    moment_new = 0.9 * moment + 0.1 * clipped
    square_new = 0.999 * square + 0.001 * clipped * clipped
    fix_one = 1.0 - 0.9**STEP
    fix_two = 1.0 - 0.999**STEP
    update = moment_new / fix_one / (jnp.sqrt(square_new / fix_two) + 1e-08) + 0.01 * weight
    weight_new = weight - rate * update
    return (weight_new, moment_new, square_new)


def on_device(
    table,
    batch_index,
    labels,
    w_branch,
    w_merge,
    w_class,
    small_params,
    first_branch,
    first_merge,
    first_class,
    first_small,
    second_branch,
    second_merge,
    second_class,
    second_small,
):
    batch = batch_index.shape[0]
    row_count = batch * lax.axis_size("dp") * lax.axis_size("rep")
    d_in = w_branch.shape[1]
    hidden = w_merge.shape[1]
    hidden_width = HOPS * hidden
    classes = w_class.shape[1]
    rows = jnp.take(table, batch_index, axis=0)
    input_features = rows.astype(jnp.bfloat16).reshape(batch, HOPS, d_in)
    branch_full, merge_full, class_full, small_full = (
        lax.all_gather(w_branch.astype(jnp.bfloat16), "dp", axis=2, tiled=True),
        lax.all_gather(w_merge.astype(jnp.bfloat16), "dp", axis=0, tiled=True),
        lax.all_gather(w_class.astype(jnp.bfloat16), "dp", axis=0, tiled=True),
        lax.all_gather(small_params.astype(jnp.bfloat16), "dp", axis=1, tiled=True),
    )
    params = small_full.astype(jnp.float32)
    gain1 = params[0:HOPS].reshape(hidden_width)
    shift1 = params[HOPS : 2 * HOPS].reshape(hidden_width)
    slope1 = params[2 * HOPS : 3 * HOPS].reshape(hidden_width)
    slope_join = params[3 * HOPS : 4 * HOPS].reshape(hidden_width)
    gain2 = params[4 * HOPS]
    shift2 = params[4 * HOPS + 1]
    slope2 = params[4 * HOPS + 2]
    bias3 = params[4 * HOPS + 3, :classes]
    first_pre = jnp.einsum(
        "fsq,sqv->fsv", input_features, branch_full, preferred_element_type=jnp.float32
    ).reshape(batch, hidden_width)
    sums_one = lax.psum(
        (jnp.sum(first_pre, axis=0), jnp.sum(first_pre * first_pre, axis=0)), ("dp", "rep")
    )
    mean1 = sums_one[0] / row_count
    inv1 = lax.rsqrt(sums_one[1] / row_count - mean1 * mean1 + EPS_NORM)
    norm1 = (first_pre - mean1) * inv1
    lin1 = gain1 * norm1 + shift1
    act1 = leaky(lin1, slope1)
    joined_low = leaky(act1, slope_join).astype(jnp.bfloat16)
    pre2 = jnp.dot(joined_low, merge_full, preferred_element_type=jnp.float32)
    sums_two = lax.psum((jnp.sum(pre2, axis=0), jnp.sum(pre2 * pre2, axis=0)), ("dp", "rep"))
    mean2 = sums_two[0] / row_count
    inv2 = lax.rsqrt(sums_two[1] / row_count - mean2 * mean2 + EPS_NORM)
    norm2 = (pre2 - mean2) * inv2
    lin2 = gain2 * norm2 + shift2
    act2_low = leaky(lin2, slope2).astype(jnp.bfloat16)
    logits = jnp.dot(act2_low, class_full, preferred_element_type=jnp.float32) + bias3
    probs = jax.nn.softmax(logits, axis=1)
    onehot = (labels[:, None] == jnp.arange(classes, dtype=jnp.int32)[None, :]).astype(jnp.float32)
    dlogits = (probs - onehot).astype(jnp.bfloat16)
    branch_back, merge_back, class_back = (
        lax.all_gather(w_branch.astype(jnp.bfloat16), "dp", axis=2, tiled=True),
        lax.all_gather(w_merge.astype(jnp.bfloat16), "dp", axis=0, tiled=True),
        lax.all_gather(w_class.astype(jnp.bfloat16), "dp", axis=0, tiled=True),
    )
    grad_class = cross_dot(act2_low, dlogits)
    grad_bias3 = jnp.sum(dlogits.astype(jnp.float32), axis=0)
    dact2 = back_dot(dlogits, class_back)
    dy2, grad_slope2 = leaky_back(dact2, lin2, slope2)
    gain2_part = jnp.sum(dy2 * norm2, axis=0)
    shift2_part = jnp.sum(dy2, axis=0)
    totals_two = lax.psum((shift2_part, gain2_part), ("dp", "rep"))
    dpre2 = (
        inv2
        * (
            gain2 * dy2
            - gain2 * totals_two[0] / row_count
            - norm2 * gain2 * totals_two[1] / row_count
        )
    ).astype(jnp.bfloat16)
    grad_merge = cross_dot(joined_low, dpre2)
    djoined = back_dot(dpre2, merge_back)
    dact1, grad_slope_join = leaky_back(djoined, act1, slope_join)
    dy1, grad_slope1 = leaky_back(dact1, lin1, slope1)
    gain1_part = jnp.sum(dy1 * norm1, axis=0)
    shift1_part = jnp.sum(dy1, axis=0)
    totals_one = lax.psum((shift1_part, gain1_part), ("dp", "rep"))
    first_grad = (
        inv1
        * (
            gain1 * dy1
            - gain1 * totals_one[0] / row_count
            - norm1 * gain1 * totals_one[1] / row_count
        )
    ).astype(jnp.bfloat16)
    first_grad = first_grad.reshape(batch, HOPS, hidden)
    branch_gradient = jnp.einsum(
        "pze,pzv->zev", input_features, first_grad, preferred_element_type=jnp.float32
    )
    row_grads = jnp.einsum(
        "fsz,sez->fse", first_grad, branch_back, preferred_element_type=jnp.float32
    ).reshape(batch, HOPS * d_in)
    bias_row = jnp.zeros((hidden,), jnp.float32).at[:classes].set(grad_bias3)
    grad_small = jnp.concatenate(
        [
            gain1_part.reshape(HOPS, hidden),
            shift1_part.reshape(HOPS, hidden),
            grad_slope1.reshape(HOPS, hidden),
            grad_slope_join.reshape(HOPS, hidden),
            gain2_part[None],
            shift2_part[None],
            grad_slope2[None],
            bias_row[None],
        ],
        axis=0,
    )
    paired = (
        lax.psum(branch_gradient.astype(jnp.bfloat16), "rep").astype(jnp.float32),
        lax.psum(grad_merge.astype(jnp.bfloat16), "rep").astype(jnp.float32),
        lax.psum(grad_class.astype(jnp.bfloat16), "rep").astype(jnp.float32),
        lax.psum(grad_small.astype(jnp.bfloat16), "rep").astype(jnp.float32),
    )
    shares = (
        lax.psum_scatter(paired[0], "dp", scatter_dimension=2, tiled=True),
        lax.psum_scatter(paired[1], "dp", scatter_dimension=0, tiled=True),
        lax.psum_scatter(paired[2], "dp", scatter_dimension=0, tiled=True),
        lax.psum_scatter(paired[3], "dp", scatter_dimension=1, tiled=True),
    )
    local_squares = jnp.float32(0.0)
    for share in shares:
        local_squares = local_squares + jnp.sum(share * share)
    grad_norm = jnp.sqrt(lax.psum(local_squares, "dp"))
    scale = 1.0 / jnp.maximum(grad_norm, 1.0)
    weights = (w_branch, w_merge, w_class, small_params)
    firsts = (first_branch, first_merge, first_class, first_small)
    seconds = (second_branch, second_merge, second_class, second_small)
    rates = (0.05, 0.05, 0.05, 0.3)
    results = [
        adamw(w, g, m, v, scale, r)
        for w, g, m, v, r in zip(weights, shares, firsts, seconds, rates)
    ]
    news = tuple((r[0] for r in results))
    moments = tuple((r[1] for r in results))
    squares = tuple((r[2] for r in results))
    copies = tuple((r.astype(jnp.bfloat16) for r in news))
    return (
        news[0],
        news[1],
        news[2],
        news[3],
        moments[0],
        moments[1],
        moments[2],
        moments[3],
        squares[0],
        squares[1],
        squares[2],
        squares[3],
        copies[0],
        copies[1],
        copies[2],
        copies[3],
        grad_norm,
        row_grads,
    )


def solution(mesh):
    placed = (
        P(("dp", "rep"), None),
        P(("dp", "rep")),
        P(("dp", "rep")),
        P(None, None, "dp"),
        P("dp", None),
        P("dp", None),
        P(None, "dp"),
        P(None, None, "dp"),
        P("dp", None),
        P("dp", None),
        P(None, "dp"),
        P(None, None, "dp"),
        P("dp", None),
        P("dp", None),
        P(None, "dp"),
    )
    return jax.shard_map(
        on_device,
        mesh=mesh,
        in_specs=placed,
        out_specs=(
            P(None, None, "dp"),
            P("dp", None),
            P("dp", None),
            P(None, "dp"),
            P(None, None, "dp"),
            P("dp", None),
            P("dp", None),
            P(None, "dp"),
            P(None, None, "dp"),
            P("dp", None),
            P("dp", None),
            P(None, "dp"),
            P(None, None, "dp"),
            P("dp", None),
            P("dp", None),
            P(None, "dp"),
            P(),
            P(("dp", "rep"), None),
        ),
        check_vma=False,
    )
```

profile of v0, /device:TPU:0, one launch (start us, length us, event | category | flops | bytes accessed | tf_op | source)
XLA Modules:
  0.0 804.2 jit_solution(16714491165405822003)
XLA Ops:
  7.2 1.6 convert_element_type.82
  8.9 0.0 all-reduce.10.cloned.1.call-start
  8.9 0.7 compare_and_fusion
  9.6 0.7 fusion.19
  10.3 0.7 convert_bitcast_fusion
  11.0 0.7 convert_element_type.84
  11.8 0.8 convert_element_type.78
  12.6 43.0 %all-gather = bf16[16,32,20]{1,2,0:T(8,128)(2,1)S(1)} all-gather(bf16[1,32,20]{1,2,0:T(8,128)(2,1)S(1)} %convert_bitcast_fusion), channel_id=1, replica_groups=mesh['dp'=16,'rep'=2] {'dp'}, dimensions={0}, use_global_device_ids=true | all-gather | bytes 21760 | tf_op jit(solution)/shard_map/all_gather | solution.py:74
  55.6 0.1 reshape.147
  55.8 40.4 %all_gather.15 = bf16[4,100,512]{1,2,0:T(8,128)(2,1)S(1)} all-gather(bf16[4,100,32]{1,2,0:T(8,128)(2,1)S(1)} %convert_element_type.78), channel_id=1, replica_groups=mesh['dp'=16,'rep'=2] {'dp'}, dimensions={2}, use_global_device_ids=true | all-gather | bytes 435200 | tf_op jit(solution)/shard_map/all_gather | solution.py:71
  96.2 6.9 copy.50
  103.1 6.7 gather_fusion
  109.8 0.5 copy.51
  110.3 0.2 gather.7
  110.5 4.5 fusion
  115.0 9.2 %copy.53 = f32[1024,2048]{1,0:T(8,128)} copy(f32[1024,2048]{0,1:T(8,128)} %bitcast.71) | data formatting | bytes 16777216 | tf_op jit(solution)/shard_map/reshape | solution.py:87
  124.2 37.0 %all-reduce.4 = (f32[2048]{0:T(1024)S(1)}, f32[2048]{0:T(1024)S(1)}) all-reduce(f32[2048]{0:T(1024)S(1)} %bitcast.97, f32[2048]{0:T(1024)S(1)} %bitcast.96), channel_id=1, replica_groups=mesh['dp'=16,'rep'=2] {'dp','rep'}, use_global_device_ids=true, to_apply=%region_3.4 | all-reduce | flops 4096 | bytes 32768 | tf_op jit(solution)/shard_map/psum | solution.py:88
  161.1 43.3 %all_gather.18 = bf16[512,47]{1,0:T(8,128)(2,1)} all-gather(bf16[32,47]{1,0:T(8,128)(2,1)S(1)} %convert_element_type.84), channel_id=1, replica_groups=mesh['dp'=16,'rep'=2] {'dp'}, dimensions={0}, use_global_device_ids=true | all-gather | bytes 51136 | tf_op jit(solution)/shard_map/all_gather | solution.py:73
  204.4 0.5 slice_bitcast_fusion.4
  204.9 0.6 fusion.31
  205.5 9.1 %add_convert_fusion = bf16[1024,2048]{1,0:T(8,128)(2,1)} fusion(f32[2048]{0:T(1024)S(1)} %get-tuple-element.89, f32[2048]{0:T(1024)S(1)} %bitcast.86, f32[2048]{0:T(1024)S(1)} %broadcast_subtract_fusion.1, f32[2048]{0:T(1024)S(1)} %bitcast.92, f32[2048]{0:T(1024)S(1)} %get-tuple-element.82, f32[1024,2048]{1,0:T(8,128)} %copy.53, ...), kind=kLoop, calls=%fused_computation.10 | loop fusion | flops 39845888 | bytes 12648448 | tf_op jit(solution)/shard_map/convert_element_type | solution.py:96
  214.7 5.2 multiply_reduce_fusion.5
  219.9 37.1 %all-reduce.3 = (f32[512]{0:T(512)}, f32[512]{0:T(512)}) all-reduce(f32[512]{0:T(512)S(1)} %get-tuple-element.40, f32[512]{0:T(512)S(1)} %get-tuple-element.39), channel_id=1, replica_groups=mesh['dp'=16,'rep'=2] {'dp','rep'}, use_global_device_ids=true, to_apply=%region_7.8 | all-reduce | flops 1024 | bytes 8192 | tf_op jit(solution)/shard_map/psum | solution.py:98
  256.9 0.7 add_rsqrt_fusion.1
  257.7 1.6 add_convert_fusion.1
  259.2 1.3 fusion.32
  260.7 1.4 fusion.30
  262.0 1.1 convolution_convert_fusion.1
  263.2 4.2 multiply_reduce_fusion.3
  267.4 0.6 copy-done.14
  268.0 0.6 convert.38
  268.6 41.4 %all-reduce.2 = (f32[512]{0:T(512)}, f32[512]{0:T(512)}) all-reduce(f32[512]{0:T(512)} %copy-done.14, f32[512]{0:T(512)} %copy-done.15), channel_id=1, replica_groups=mesh['dp'=16,'rep'=2] {'dp','rep'}, use_global_device_ids=true, to_apply=%region_13.14 | all-reduce | flops 1024 | bytes 8192 | tf_op jit(solution)/shard_map/psum | solution.py:119
  310.0 0.8 multiply_multiply_fusion.5
  310.9 2.7 multiply_convert_fusion.1
  313.6 3.8 convolution_convert_fusion
  317.4 13.9 %multiply_reduce_fusion = (bf16[2048]{0:T(1024)(128)(2,1)S(1)}, bf16[2048]{0:T(1024)(128)(2,1)S(1)}, f32[2048]{0:T(1024)S(1)}, f32[2048]{0:T(1024)S(1)}, f32[1024,2048]{1,0:T(8,128)}) fusion(f32[2048]{0:T(1024)S(1)} %broadcast_subtract_fusion.1, f32[2048]{0:T(1024)S(1)} %bitcast.93, f32[2048]{0:T(1024)S(1)} %get-tuple-element.82, ...), kind=kOutput, calls=%fused_computation.4 | convolution fusion | flops 2225070080 | bytes 20013056 | tf_op jit(solution)/shard_map/dot_general | solution.py:29
  331.3 40.2 %all-reduce.1 = (f32[2048]{0:T(1024)S(1)}, f32[2048]{0:T(1024)S(1)}) all-reduce(f32[2048]{0:T(1024)S(1)} %get-tuple-element.32, f32[2048]{0:T(1024)S(1)} %get-tuple-element.33), channel_id=1, replica_groups=mesh['dp'=16,'rep'=2] {'dp','rep'}, use_global_device_ids=true, to_apply=%region_17.18 | all-reduce | flops 4096 | bytes 32768 | tf_op jit(solution)/shard_map/psum | solution.py:134
  371.7 1.9 concatenate.6
  373.5 0.3 all-reduce.12.cloned.1.call-start
  373.8 7.3 multiply_convert_fusion
  381.1 1.9 copy-done
  383.0 2.5 fusion.10
  385.6 5.8 all-reduce.10.cloned.1.call-done
  391.4 1.6 copy.56
  393.1 1.6 convert_element_type.94
  394.8 23.1 %all-reduce.12.cloned.1.call-done = (bf16[4,100,512]{1,2,0:T(8,128)(2,1)}, bf16[2048,512]{1,0:T(8,128)(2,1)}) async-done(((bf16[4,100,512]{1,2,0:T(8,128)(2,1)}, bf16[2048,512]{1,0:T(8,128)(2,1)}), (bf16[4,100,512]{1,2,0:T(8,128)(2,1)}, bf16[2048,512]{1,0:T(8,128)(2,1)})) %all-reduce.12.cloned.1.call-update) | async-done | bytes 2506768 | tf_op jit(solution)/shard_map/psum | solution.py:165
  417.9 2.1 convert_element_type.90
  420.1 4.2 convert_element_type.92
  424.4 3.7 fusion.7
  428.1 69.9 %reduce-scatter.13.cloned.1.call-done = f32[32,20]{1,0:T(8,128)} async-done(((f32[512,20]{1,0:T(8,128)}), f32[32,20]{1,0:T(8,128)}) %reduce-scatter.13.cloned.1.call-update) | async-done | bytes 2576
  498.0 0.8 copy.57
  498.8 0.6 multiply_reduce_fusion.9
  499.4 73.8 %reduce-scatter.11.cloned.1.call-done = f32[32,47]{1,0:T(8,128)} async-done(((f32[512,47]{1,0:T(8,128)}), f32[32,47]{1,0:T(8,128)}) %reduce-scatter.11.cloned.1.call-update) | async-done | bytes 6032 | tf_op jit(solution)/shard_map/reduce_scatter | solution.py:173
  573.1 1.3 multiply_reduce_fusion.8
  574.5 75.5 %reduce-scatter.7.cloned.1.call-done = f32[4,100,32]{1,2,0:T(8,128)} async-done(((f32[4,100,512]{1,2,0:T(8,128)}), f32[4,100,32]{1,2,0:T(8,128)}) %reduce-scatter.7.cloned.1.call-update) | async-done | bytes 51216 | tf_op jit(solution)/shard_map/reduce_scatter | solution.py:171
  650.0 1.5 multiply_reduce_fusion.7
  651.5 92.4 %reduce-scatter.9.cloned.1.call-done = f32[128,512]{1,0:T(8,128)} async-done(((f32[2048,512]{1,0:T(8,128)}), f32[128,512]{1,0:T(8,128)}) %reduce-scatter.9.cloned.1.call-update) | async-done | bytes 262160 | tf_op jit(solution)/shard_map/reduce_scatter | solution.py:172
  743.9 1.7 multiply_reduce_fusion.6
  748.2 1.3 reshape.135
  749.5 40.5 %psum.103 = f32[]{:T(128)} all-reduce(f32[]{:T(128)S(6)} %add.234), channel_id=1, replica_groups=mesh['dp'=16,'rep'=2] {'dp'}, use_global_device_ids=true, to_apply=%region_34.35 | all-reduce | flops 1 | bytes 8 | tf_op jit(solution)/shard_map/psum | solution.py:179
  790.8 1.4 fusion.22
  792.2 1.4 fusion.24
  793.5 1.6 fusion.28
  795.1 1.1 fusion.26
  (83 shorter events, 0.6 us)
Async XLA Ops:
  7.2 207.5 %all-gather.3.cloned.1.call-start = ((), (), s32[]{:S(2)}) async-start(), calls=%async_computation.4 | async-start | bytes 2228224 | tf_op jit(solution)/shard_map/all_gather | solution.py:72
  8.9 382.5 %all-reduce.10.cloned.1.call-start = ((), (), s32[]{:S(2)}) async-start(), calls=%async_computation.9 | async-start | bytes 311296 | tf_op jit(solution)/shard_map/psum | solution.py:167
  9.6 100.9 %copy-start.16 = (pred[1024]{0:T(1024)(128)(4,1)}, pred[1024]{0:T(1024)(128)(4,1)S(1)}, u32[]{:S(2)}) copy-start(pred[1024]{0:T(1024)(128)(4,1)S(1)} %compare_and_fusion) | copy-start | bytes 3076
  256.9 6.2 copy-start.4
  267.4 0.6 copy-start.14
  267.4 1.1 copy-start.15
  310.0 3.5 copy-start.1
  310.8 6.5 slice-start
  313.5 3.8 slice-start.1
  313.6 3.8 copy-start.21
  317.4 54.2 %copy-start.20 = (bf16[512]{0:T(512)(128)(2,1)S(1)}, bf16[512]{0:T(512)(128)(2,1)}, u32[]{:S(2)}) copy-start(bf16[512]{0:T(512)(128)(2,1)} %get-tuple-element.36) | copy-start | bytes 3076
  317.4 54.2 %copy-start.18 = (bf16[512]{0:T(512)(128)(2,1)S(1)}, bf16[512]{0:T(512)(128)(2,1)}, u32[]{:S(2)}) copy-start(bf16[512]{0:T(512)(128)(2,1)} %convert.38) | copy-start | bytes 3076
  317.4 54.2 %copy-start.19 = (bf16[47]{0:T(256)(128)(2,1)S(1)}, bf16[47]{0:T(256)(128)(2,1)}, u32[]{:S(2)}) copy-start(bf16[47]{0:T(256)(128)(2,1)} %get-tuple-element.69) | copy-start | bytes 286
  373.5 44.4 %all-reduce.12.cloned.1.call-start = ((), (), s32[]{:S(2)}) async-start(), calls=%async_computation.10 | async-start | bytes 5242880 | tf_op jit(solution)/shard_map/psum | solution.py:165
  373.8 9.2 %copy-start.17 = (pred[1024]{0:T(1024)(128)(4,1)S(1)}, pred[1024]{0:T(1024)(128)(4,1)}, u32[]{:S(2)}) copy-start(pred[1024]{0:T(1024)(128)(4,1)} %copy-done.16) | copy-start | bytes 3076
  381.1 1.9 copy-start
  385.5 112.5 %reduce-scatter.13.cloned.1.call-start = ((), (), s32[]{:S(2)}) async-start(), calls=%async_computation.8 | async-start | bytes 278528
  393.0 180.1 %reduce-scatter.11.cloned.1.call-start = ((), (), s32[]{:S(2)}) async-start(), calls=%async_computation.7 | async-start | bytes 278528 | tf_op jit(solution)/shard_map/reduce_scatter | solution.py:173
  394.7 255.3 %reduce-scatter.7.cloned.1.call-start = ((), (), s32[]{:S(2)}) async-start(), calls=%async_computation.5 | async-start | bytes 1114112 | tf_op jit(solution)/shard_map/reduce_scatter | solution.py:171
  420.0 323.9 %reduce-scatter.9.cloned.1.call-start = ((), (), s32[]{:S(2)}) async-start(), calls=%async_computation.6 | async-start | bytes 4456448 | tf_op jit(solution)/shard_map/reduce_scatter | solution.py:172
  424.2 366.6 %copy-start.11 = (f32[20,32]{1,0:T(8,128)S(1)}, f32[20,32]{1,0:T(8,128)}, u32[]{:S(2)}) copy-start(f32[20,32]{1,0:T(8,128)} %param.23) | copy-start | bytes 7684
  424.2 367.9 %copy-start.10 = (f32[32,47]{1,0:T(8,128)S(1)}, f32[32,47]{1,0:T(8,128)}, u32[]{:S(2)}) copy-start(f32[32,47]{1,0:T(8,128)} %param.22) | copy-start | bytes 18052
  424.3 367.9 %copy-start.12 = (f32[32,47]{1,0:T(8,128)S(1)}, f32[32,47]{1,0:T(8,128)}, u32[]{:S(2)}) copy-start(f32[32,47]{1,0:T(8,128)} %param.26) | copy-start | bytes 18052
  424.3 367.9 %copy-start.13 = (f32[32,47]{1,0:T(8,128)S(1)}, f32[32,47]{1,0:T(8,128)}, u32[]{:S(2)}) copy-start(f32[32,47]{1,0:T(8,128)} %param.30) | copy-start | bytes 18052
  424.3 369.3 %copy-start.7 = (f32[4,100,32]{1,2,0:T(8,128)S(1)}, f32[4,100,32]{1,2,0:T(8,128)}, u32[]{:S(2)}) copy-start(f32[4,100,32]{1,2,0:T(8,128)} %param.20) | copy-start | bytes 153604
  424.3 369.2 %copy-start.8 = (f32[4,100,32]{1,2,0:T(8,128)S(1)}, f32[4,100,32]{1,2,0:T(8,128)}, u32[]{:S(2)}) copy-start(f32[4,100,32]{1,2,0:T(8,128)} %param.24) | copy-start | bytes 153604
  424.3 369.2 %copy-start.9 = (f32[4,100,32]{1,2,0:T(8,128)S(1)}, f32[4,100,32]{1,2,0:T(8,128)}, u32[]{:S(2)}) copy-start(f32[4,100,32]{1,2,0:T(8,128)} %param.28) | copy-start | bytes 153604
  424.3 370.8 %copy-start.2 = (f32[128,512]{1,0:T(8,128)S(1)}, f32[128,512]{1,0:T(8,128)}, u32[]{:S(2)}) copy-start(f32[128,512]{1,0:T(8,128)} %param.21) | copy-start | bytes 786436
  424.3 370.8 %copy-start.5 = (f32[128,512]{1,0:T(8,128)S(1)}, f32[128,512]{1,0:T(8,128)}, u32[]{:S(2)}) copy-start(f32[128,512]{1,0:T(8,128)} %param.25) | copy-start | bytes 786436
  424.3 370.8 %copy-start.6 = (f32[128,512]{1,0:T(8,128)S(1)}, f32[128,512]{1,0:T(8,128)}, u32[]{:S(2)}) copy-start(f32[128,512]{1,0:T(8,128)} %param.29) | copy-start | bytes 786436
  743.9 51.2 %copy-start.3 = (f32[128,512]{1,0:T(8,128)S(1)}, f32[128,512]{1,0:T(8,128)}, u32[]{:S(2)}) copy-start(f32[128,512]{1,0:T(8,128)} %reduce-scatter.9.cloned.1.call-done) | copy-start | bytes 786436
Sparse Core Ops, SparseCore 0:
  11.4 66.4 all-gather.2
  373.7 17.7 all-reduce.9
  394.4 23.4 all-reduce.11
  420.7 77.2 reduce-scatter.12
  500.6 72.4 reduce-scatter.10
  575.9 74.0 reduce-scatter.6
  652.3 91.5 reduce-scatter.8
where the time goes:
time: 806 us; the launch traced here: 804 us
  waiting for transfers between devices  341 us (42%)
  blocking collectives  323 us (40%)
  other arithmetic  48.4 us (6%)
  matrix products  40.3 us (5%)
  local copies, waits for them, and re-layouts  32.3 us (4%)
  between operations  19 us (2%)
    reduce_scatter x1, waiting for transfers between devices, on_device(): lax.psum_scatter(paired[1], 'dp', scatter_dimension=0, tiled=True)  92.4 us
    reduce_scatter x1, waiting for transfers between devices, on_device(): lax.psum_scatter(paired[0], 'dp', scatter_dimension=2, tiled=True)  75.5 us
    reduce_scatter x1, waiting for transfers between devices, on_device(): lax.psum_scatter(paired[2], 'dp', scatter_dimension=0, tiled=True)  73.8 us
    unnamed x8, waiting for transfers between devices  70 us
    all_gather x1, blocking collectives, on_device(): lax.all_gather(w_class.astype(jnp.bfloat16), 'dp', axis=0, tiled=True)  43.3 us
    all_gather x1, blocking collectives, on_device(): lax.all_gather(small_params.astype(jnp.bfloat16), 'dp', axis=1, tiled=True)  43 us
    psum x1, blocking collectives, on_device(): totals_two = lax.psum((shift2_part, gain2_part), ('dp', 'rep'))  41.4 us
    psum x1, blocking collectives, on_device(): grad_norm = jnp.sqrt(lax.psum(local_squares, 'dp'))  40.5 us
  transfers between devices with their start and end apart: 7, of which 6 were waited for; matrix products, arithmetic and copies ran while one was open for 9% of the time, Pallas kernels for 0%

commit v1 on v0

--- a/solution.py
+++ b/solution.py
@@ -86,7 +86,7 @@
         "fsq,sqv->fsv", input_features, branch_full, preferred_element_type=jnp.float32
     ).reshape(batch, hidden_width)
     sums_one = lax.psum(
-        (jnp.sum(first_pre, axis=0), jnp.sum(first_pre * first_pre, axis=0)), ("dp", "rep")
+        lax.psum((jnp.sum(first_pre, axis=0), jnp.sum(first_pre * first_pre, axis=0)), "rep"), "dp"
     )
     mean1 = sums_one[0] / row_count
     inv1 = lax.rsqrt(sums_one[1] / row_count - mean1 * mean1 + EPS_NORM)

time: 806 us -> 842 us (1.045)
  blocking collectives: 323 us -> 358 us
    psum x0 -> x1, blocking collectives: none -> 72.9 us  [on_device(): lax.psum(lax.psum((jnp.sum(first_pre, axis=0), jnp.sum(first_pre * first_...]
    psum x1, blocking collectives: 37 us -> 3.28 us  [on_device(): lax.psum((jnp.sum(first_pre, axis=0), jnp.sum(first_pre * first_pre, axis...]
  transfers between devices with their start and end apart: 7 -> 7, of which waited for: 6 -> 6; matrix products, arithmetic and copies ran while one was open for 9% -> 8% of each run, Pallas kernels for 0% -> 0%
where the time goes in v1:
time: 842 us; the launch traced here: 840 us
  blocking collectives  358 us (43%)
  waiting for transfers between devices  342 us (41%)
  other arithmetic  48.3 us (6%)
  matrix products  40.3 us (5%)
  local copies, waits for them, and re-layouts  32.3 us (4%)
  between operations  19 us (2%)
    reduce_scatter x1, waiting for transfers between devices, on_device(): lax.psum_scatter(paired[1], 'dp', scatter_dimension=0, tiled=True)  92.4 us
    reduce_scatter x1, waiting for transfers between devices, on_device(): lax.psum_scatter(paired[0], 'dp', scatter_dimension=2, tiled=True)  75.5 us
    reduce_scatter x1, waiting for transfers between devices, on_device(): lax.psum_scatter(paired[2], 'dp', scatter_dimension=0, tiled=True)  73.8 us
    psum x1, blocking collectives, on_device(): lax.psum(lax.psum((jnp.sum(first_pre, axis=0), jnp.sum(first_pre * first_...  72.9 us
    unnamed x8, waiting for transfers between devices  70 us
    psum x1, blocking collectives, on_device(): totals_two = lax.psum((shift2_part, gain2_part), ('dp', 'rep'))  43.3 us
    all_gather x1, blocking collectives, on_device(): lax.all_gather(small_params.astype(jnp.bfloat16), 'dp', axis=1, tiled=True)  43 us
    psum x1, blocking collectives, on_device(): grad_norm = jnp.sqrt(lax.psum(local_squares, 'dp'))  40.5 us
  transfers between devices with their start and end apart: 7, of which 6 were waited for; matrix products, arithmetic and copies ran while one was open for 8% of the time, Pallas kernels for 0%

profile of v1, /device:TPU:0, one launch (start us, length us, event | category | flops | bytes accessed | tf_op | source)
XLA Modules:
  0.0 840.0 jit_solution(15525753565361994493)
XLA Ops:
  7.2 1.6 convert_element_type.82
  8.9 0.7 compare_and_fusion
  9.6 0.7 fusion.19
  10.3 0.7 convert_bitcast_fusion
  11.0 0.7 convert_element_type.84
  11.8 0.8 convert_element_type.78
  12.6 43.0 %all-gather = bf16[16,32,20]{1,2,0:T(8,128)(2,1)S(1)} all-gather(bf16[1,32,20]{1,2,0:T(8,128)(2,1)S(1)} %convert_bitcast_fusion), channel_id=1, replica_groups=mesh['dp'=16,'rep'=2] {'dp'}, dimensions={0}, use_global_device_ids=true | all-gather | bytes 21760 | tf_op jit(solution)/shard_map/all_gather | solution.py:74
  55.6 0.1 reshape.147
  55.8 40.4 %all_gather.15 = bf16[4,100,512]{1,2,0:T(8,128)(2,1)S(1)} all-gather(bf16[4,100,32]{1,2,0:T(8,128)(2,1)S(1)} %convert_element_type.78), channel_id=1, replica_groups=mesh['dp'=16,'rep'=2] {'dp'}, dimensions={2}, use_global_device_ids=true | all-gather | bytes 435200 | tf_op jit(solution)/shard_map/all_gather | solution.py:71
  96.2 6.9 copy.50
  103.1 6.7 gather_fusion
  109.8 0.5 copy.51
  110.3 0.2 gather.7
  110.5 4.5 fusion
  115.0 9.2 %copy.53 = f32[1024,2048]{1,0:T(8,128)} copy(f32[1024,2048]{0,1:T(8,128)} %bitcast.71) | data formatting | bytes 16777216 | tf_op jit(solution)/shard_map/reshape | solution.py:87
  124.2 3.3 all-reduce.5
  127.4 72.9 %all-reduce.4 = (f32[2048]{0:T(1024)S(1)}, f32[2048]{0:T(1024)S(1)}) all-reduce(f32[2048]{0:T(1024)S(1)} %get-tuple-element.49, f32[2048]{0:T(1024)S(1)} %get-tuple-element.50), channel_id=1, replica_groups=mesh['dp'=16,'rep'=2] {'dp'}, use_global_device_ids=true, to_apply=%region_5.6 | all-reduce | flops 4096 | bytes 32768 | tf_op jit(solution)/shard_map/psum | solution.py:88
  200.4 38.5 %all_gather.18 = bf16[512,47]{1,0:T(8,128)(2,1)} all-gather(bf16[32,47]{1,0:T(8,128)(2,1)S(1)} %convert_element_type.84), channel_id=1, replica_groups=mesh['dp'=16,'rep'=2] {'dp'}, dimensions={0}, use_global_device_ids=true | all-gather | bytes 51136 | tf_op jit(solution)/shard_map/all_gather | solution.py:73
  238.8 0.5 slice_bitcast_fusion.4
  239.3 0.6 fusion.31
  239.9 9.1 %add_convert_fusion = bf16[1024,2048]{1,0:T(8,128)(2,1)} fusion(f32[2048]{0:T(1024)S(1)} %get-tuple-element.91, f32[2048]{0:T(1024)S(1)} %bitcast.86, f32[2048]{0:T(1024)S(1)} %broadcast_subtract_fusion.1, f32[2048]{0:T(1024)S(1)} %bitcast.92, f32[2048]{0:T(1024)S(1)} %get-tuple-element.84, f32[1024,2048]{1,0:T(8,128)} %copy.53, ...), kind=kLoop, calls=%fused_computation.10 | loop fusion | flops 39845888 | bytes 12648448 | tf_op jit(solution)/shard_map/convert_element_type | solution.py:96
  249.1 5.2 multiply_reduce_fusion.5
  254.3 37.1 %all-reduce.3 = (f32[512]{0:T(512)}, f32[512]{0:T(512)}) all-reduce(f32[512]{0:T(512)S(1)} %get-tuple-element.40, f32[512]{0:T(512)S(1)} %get-tuple-element.39), channel_id=1, replica_groups=mesh['dp'=16,'rep'=2] {'dp','rep'}, use_global_device_ids=true, to_apply=%region_9.10 | all-reduce | flops 1024 | bytes 8192 | tf_op jit(solution)/shard_map/psum | solution.py:98
  291.4 0.7 add_rsqrt_fusion.1
  292.1 1.6 add_convert_fusion.1
  293.7 1.3 fusion.32
  295.1 1.4 fusion.30
  296.4 1.1 convolution_convert_fusion.1
  297.6 4.2 multiply_reduce_fusion.3
  301.8 0.6 copy-done.14
  302.4 0.6 convert.38
  303.0 43.3 %all-reduce.2 = (f32[512]{0:T(512)}, f32[512]{0:T(512)}) all-reduce(f32[512]{0:T(512)} %copy-done.14, f32[512]{0:T(512)} %copy-done.15), channel_id=1, replica_groups=mesh['dp'=16,'rep'=2] {'dp','rep'}, use_global_device_ids=true, to_apply=%region_15.16 | all-reduce | flops 1024 | bytes 8192 | tf_op jit(solution)/shard_map/psum | solution.py:119
  346.3 0.8 multiply_multiply_fusion.5
  347.2 2.7 multiply_convert_fusion.1
  349.9 3.8 convolution_convert_fusion
  353.7 13.9 %multiply_reduce_fusion = (bf16[2048]{0:T(1024)(128)(2,1)S(1)}, bf16[2048]{0:T(1024)(128)(2,1)S(1)}, f32[2048]{0:T(1024)S(1)}, f32[2048]{0:T(1024)S(1)}, f32[1024,2048]{1,0:T(8,128)}) fusion(f32[2048]{0:T(1024)S(1)} %broadcast_subtract_fusion.1, f32[2048]{0:T(1024)S(1)} %bitcast.93, f32[2048]{0:T(1024)S(1)} %get-tuple-element.84, ...), kind=kOutput, calls=%fused_computation.4 | convolution fusion | flops 2225070080 | bytes 20013056 | tf_op jit(solution)/shard_map/dot_general | solution.py:29
  367.6 38.5 %all-reduce.1 = (f32[2048]{0:T(1024)S(1)}, f32[2048]{0:T(1024)S(1)}) all-reduce(f32[2048]{0:T(1024)S(1)} %get-tuple-element.32, f32[2048]{0:T(1024)S(1)} %get-tuple-element.33), channel_id=1, replica_groups=mesh['dp'=16,'rep'=2] {'dp','rep'}, use_global_device_ids=true, to_apply=%region_19.20 | all-reduce | flops 4096 | bytes 32768 | tf_op jit(solution)/shard_map/psum | solution.py:134
  406.2 1.9 concatenate.6
  408.1 0.3 all-reduce.13.cloned.1.call-start
  408.4 7.2 multiply_convert_fusion
  415.6 1.9 copy-done
  417.6 2.5 fusion.10
  420.1 7.2 all-reduce.11.cloned.1.call-done
  427.3 1.6 copy.56
  428.9 1.6 convert_element_type.94
  430.6 23.1 %all-reduce.13.cloned.1.call-done = (bf16[4,100,512]{1,2,0:T(8,128)(2,1)}, bf16[2048,512]{1,0:T(8,128)(2,1)}) async-done(((bf16[4,100,512]{1,2,0:T(8,128)(2,1)}, bf16[2048,512]{1,0:T(8,128)(2,1)}), (bf16[4,100,512]{1,2,0:T(8,128)(2,1)}, bf16[2048,512]{1,0:T(8,128)(2,1)})) %all-reduce.13.cloned.1.call-update) | async-done | bytes 2506768 | tf_op jit(solution)/shard_map/psum | solution.py:165
  453.7 2.1 convert_element_type.90
  455.9 4.2 convert_element_type.92
  460.2 3.7 fusion.7
  463.9 69.9 %reduce-scatter.13.cloned.1.call-done = f32[32,20]{1,0:T(8,128)} async-done(((f32[512,20]{1,0:T(8,128)}), f32[32,20]{1,0:T(8,128)}) %reduce-scatter.13.cloned.1.call-update) | async-done | bytes 2576
  533.8 0.8 copy.57
  534.6 0.6 multiply_reduce_fusion.9
  535.2 73.8 %reduce-scatter.11.cloned.1.call-done = f32[32,47]{1,0:T(8,128)} async-done(((f32[512,47]{1,0:T(8,128)}), f32[32,47]{1,0:T(8,128)}) %reduce-scatter.11.cloned.1.call-update) | async-done | bytes 6032 | tf_op jit(solution)/shard_map/reduce_scatter | solution.py:173
  609.0 1.3 multiply_reduce_fusion.8
  610.3 75.5 %reduce-scatter.7.cloned.1.call-done = f32[4,100,32]{1,2,0:T(8,128)} async-done(((f32[4,100,512]{1,2,0:T(8,128)}), f32[4,100,32]{1,2,0:T(8,128)}) %reduce-scatter.7.cloned.1.call-update) | async-done | bytes 51216 | tf_op jit(solution)/shard_map/reduce_scatter | solution.py:171
  685.8 1.5 multiply_reduce_fusion.7
  687.3 92.4 %reduce-scatter.9.cloned.1.call-done = f32[128,512]{1,0:T(8,128)} async-done(((f32[2048,512]{1,0:T(8,128)}), f32[128,512]{1,0:T(8,128)}) %reduce-scatter.9.cloned.1.call-update) | async-done | bytes 262160 | tf_op jit(solution)/shard_map/reduce_scatter | solution.py:172
  779.7 1.7 multiply_reduce_fusion.6
  784.0 1.3 reshape.135
  785.4 40.5 %psum.119 = f32[]{:T(128)} all-reduce(f32[]{:T(128)S(6)} %add.238), channel_id=1, replica_groups=mesh['dp'=16,'rep'=2] {'dp'}, use_global_device_ids=true, to_apply=%region_36.37 | all-reduce | flops 1 | bytes 8 | tf_op jit(solution)/shard_map/psum | solution.py:179
  826.6 1.4 fusion.22
  828.0 1.4 fusion.24
  829.4 1.6 fusion.28
  831.0 1.1 fusion.26
  (84 shorter events, 0.7 us)
Async XLA Ops:
  7.2 241.9 %all-gather.3.cloned.1.call-start = ((), (), s32[]{:S(2)}) async-start(), calls=%async_computation.4 | async-start | bytes 2228224 | tf_op jit(solution)/shard_map/all_gather | solution.py:72
  8.9 418.4 %all-reduce.11.cloned.1.call-start = ((), (), s32[]{:S(2)}) async-start(), calls=%async_computation.9 | async-start | bytes 311296 | tf_op jit(solution)/shard_map/psum | solution.py:167
  9.6 100.9 %copy-start.16 = (pred[1024]{0:T(1024)(128)(4,1)}, pred[1024]{0:T(1024)(128)(4,1)S(1)}, u32[]{:S(2)}) copy-start(pred[1024]{0:T(1024)(128)(4,1)S(1)} %compare_and_fusion) | copy-start | bytes 3076
  291.3 6.2 copy-start.4
  301.8 0.6 copy-start.14
  301.8 1.1 copy-start.15
  346.3 3.5 copy-start.1
  347.2 6.5 slice-start
  349.8 3.8 slice-start.1
  349.9 3.8 copy-start.21
  353.7 52.4 %copy-start.20 = (bf16[512]{0:T(512)(128)(2,1)S(1)}, bf16[512]{0:T(512)(128)(2,1)}, u32[]{:S(2)}) copy-start(bf16[512]{0:T(512)(128)(2,1)} %get-tuple-element.36) | copy-start | bytes 3076
  353.7 52.4 %copy-start.18 = (bf16[512]{0:T(512)(128)(2,1)S(1)}, bf16[512]{0:T(512)(128)(2,1)}, u32[]{:S(2)}) copy-start(bf16[512]{0:T(512)(128)(2,1)} %convert.38) | copy-start | bytes 3076
  353.7 52.5 %copy-start.19 = (bf16[47]{0:T(256)(128)(2,1)S(1)}, bf16[47]{0:T(256)(128)(2,1)}, u32[]{:S(2)}) copy-start(bf16[47]{0:T(256)(128)(2,1)} %get-tuple-element.71) | copy-start | bytes 286
  408.1 45.6 %all-reduce.13.cloned.1.call-start = ((), (), s32[]{:S(2)}) async-start(), calls=%async_computation.10 | async-start | bytes 5242880 | tf_op jit(solution)/shard_map/psum | solution.py:165
  408.4 9.2 %copy-start.17 = (pred[1024]{0:T(1024)(128)(4,1)S(1)}, pred[1024]{0:T(1024)(128)(4,1)}, u32[]{:S(2)}) copy-start(pred[1024]{0:T(1024)(128)(4,1)} %copy-done.16) | copy-start | bytes 3076
  415.6 1.9 copy-start
  420.0 113.8 %reduce-scatter.13.cloned.1.call-start = ((), (), s32[]{:S(2)}) async-start(), calls=%async_computation.8 | async-start | bytes 278528
  428.8 180.1 %reduce-scatter.11.cloned.1.call-start = ((), (), s32[]{:S(2)}) async-start(), calls=%async_computation.7 | async-start | bytes 278528 | tf_op jit(solution)/shard_map/reduce_scatter | solution.py:173
  430.5 255.3 %reduce-scatter.7.cloned.1.call-start = ((), (), s32[]{:S(2)}) async-start(), calls=%async_computation.5 | async-start | bytes 1114112 | tf_op jit(solution)/shard_map/reduce_scatter | solution.py:171
  455.8 323.9 %reduce-scatter.9.cloned.1.call-start = ((), (), s32[]{:S(2)}) async-start(), calls=%async_computation.6 | async-start | bytes 4456448 | tf_op jit(solution)/shard_map/reduce_scatter | solution.py:172
  460.1 366.6 %copy-start.11 = (f32[20,32]{1,0:T(8,128)S(1)}, f32[20,32]{1,0:T(8,128)}, u32[]{:S(2)}) copy-start(f32[20,32]{1,0:T(8,128)} %param.23) | copy-start | bytes 7684
  460.1 367.9 %copy-start.10 = (f32[32,47]{1,0:T(8,128)S(1)}, f32[32,47]{1,0:T(8,128)}, u32[]{:S(2)}) copy-start(f32[32,47]{1,0:T(8,128)} %param.22) | copy-start | bytes 18052
  460.1 367.9 %copy-start.12 = (f32[32,47]{1,0:T(8,128)S(1)}, f32[32,47]{1,0:T(8,128)}, u32[]{:S(2)}) copy-start(f32[32,47]{1,0:T(8,128)} %param.26) | copy-start | bytes 18052
  460.1 367.9 %copy-start.13 = (f32[32,47]{1,0:T(8,128)S(1)}, f32[32,47]{1,0:T(8,128)}, u32[]{:S(2)}) copy-start(f32[32,47]{1,0:T(8,128)} %param.30) | copy-start | bytes 18052
  460.1 369.3 %copy-start.7 = (f32[4,100,32]{1,2,0:T(8,128)S(1)}, f32[4,100,32]{1,2,0:T(8,128)}, u32[]{:S(2)}) copy-start(f32[4,100,32]{1,2,0:T(8,128)} %param.20) | copy-start | bytes 153604
  460.1 369.2 %copy-start.8 = (f32[4,100,32]{1,2,0:T(8,128)S(1)}, f32[4,100,32]{1,2,0:T(8,128)}, u32[]{:S(2)}) copy-start(f32[4,100,32]{1,2,0:T(8,128)} %param.24) | copy-start | bytes 153604
  460.1 369.2 %copy-start.9 = (f32[4,100,32]{1,2,0:T(8,128)S(1)}, f32[4,100,32]{1,2,0:T(8,128)}, u32[]{:S(2)}) copy-start(f32[4,100,32]{1,2,0:T(8,128)} %param.28) | copy-start | bytes 153604
  460.2 370.8 %copy-start.2 = (f32[128,512]{1,0:T(8,128)S(1)}, f32[128,512]{1,0:T(8,128)}, u32[]{:S(2)}) copy-start(f32[128,512]{1,0:T(8,128)} %param.21) | copy-start | bytes 786436
  460.2 370.8 %copy-start.5 = (f32[128,512]{1,0:T(8,128)S(1)}, f32[128,512]{1,0:T(8,128)}, u32[]{:S(2)}) copy-start(f32[128,512]{1,0:T(8,128)} %param.25) | copy-start | bytes 786436
  460.2 370.8 %copy-start.6 = (f32[128,512]{1,0:T(8,128)S(1)}, f32[128,512]{1,0:T(8,128)}, u32[]{:S(2)}) copy-start(f32[128,512]{1,0:T(8,128)} %param.29) | copy-start | bytes 786436
  779.7 51.2 %copy-start.3 = (f32[128,512]{1,0:T(8,128)S(1)}, f32[128,512]{1,0:T(8,128)}, u32[]{:S(2)}) copy-start(f32[128,512]{1,0:T(8,128)} %reduce-scatter.9.cloned.1.call-done) | copy-start | bytes 786436
Sparse Core Ops, SparseCore 0:
  11.4 66.4 all-gather.2
  408.2 18.9 all-reduce.10
  430.2 23.4 all-reduce.12
  456.5 77.2 reduce-scatter.12
  536.5 72.4 reduce-scatter.10
  611.8 74.0 reduce-scatter.6
  688.1 91.5 reduce-scatter.8
